TPU v7x, 256 devices: a whole 4x4x8 slice. The times are simulated.
256 devices in a mesh: gen: 8 (over z_lo, core), user: 16 (over x, y), cand: 2 (over z_hi).
Axes of the slice: x: 4, y: 4, z: 8 (z_hi: 2, z_lo: 4; z = z_hi * 4 + z_lo), core: 2. Of those that a mesh axis runs over, the one named last changes fastest.
Arguments:
- states: bfloat16 [16384, 4096], P(('user', 'cand')), may hold values from -6 to 6
- norm_gain: float32 [4096], replicated, may hold values from 0.1 to 1.9
- gate_weight: bfloat16 [4096, 7168], P('user', 'gen'), may hold values from -0.09375 to 0.09375
- up_weight: bfloat16 [4096, 7168], P('user', 'gen'), may hold values from -0.09375 to 0.09375
- down_weight: bfloat16 [7168, 4096], P('gen', 'user'), may hold values from -0.0625 to 0.0625
- proj_weight: bfloat16 [4096, 1024], P('gen'), may hold values from -0.09375 to 0.09375
- private_rows: bfloat16 [32768, 1024], P(('gen', 'user')), may hold values from -6 to 6
- enc_weight: bfloat16 [1024, 1024], replicated, may hold values from -0.1875 to 0.1875
- user_ids: int32 [32768], P(('gen', 'user')), may hold values from 0 to 31
Outputs:
- votes: float32 [16, 2, 128], P(None, 'cand')
Inputs may be any that keep to these rules, and one draw needn't show every extreme that they name: `user_ids`: a user is a pair of a block of 256 rows and a slot; no user has rows in two blocks.
All inputs are finite; a program needn't handle non-finite values.
Results may differ from a plain program's by a relative error of at most 0.0025.
Values may be sent and summed in bfloat16 or wider, within the bound.
No kernel may reach another device: no remote copies, remote signals or barrier semaphores. Data moves between devices by JAX's collectives and lax.ppermute only.
A program may use at most 128 MiB of HBM per device.

v0:
```python
import jax
import jax.numpy as jnp
from jax import lax
from jax.sharding import PartitionSpec as P

STEPS = 4
CAP = 8
USERS_DEV = 32


def unit_rows(matrix):
    return (matrix * lax.rsqrt(jnp.sum(matrix * matrix, axis=1, keepdims=True) + 1e-06)).astype(
        jnp.bfloat16
    )


def project_in(inputs, gate_part, up_part):

    def add_rows(piece):
        return jnp.dot(inputs, piece, preferred_element_type=jnp.float32)

    gate = add_rows(lax.all_gather(gate_part, "user", axis=0, tiled=True))
    up_proj = add_rows(lax.all_gather(up_part, "user", axis=0, tiled=True))
    return (gate, up_proj)


def shards(
    states,
    norm_gain,
    gate_weight,
    up_weight,
    down_weight,
    proj_weight,
    private_rows,
    enc_weight,
    user_ids,
):
    tok_rows, width_model = states.shape
    groups = tok_rows // STEPS
    values = states.astype(jnp.float32)
    normed = (
        values * lax.rsqrt(jnp.mean(values * values, axis=1, keepdims=True) + 1e-05) * norm_gain
    ).astype(jnp.bfloat16)
    gate_part, up_part, down_part = (gate_weight, up_weight, down_weight)
    gate, up_proj = project_in(normed, gate_part, up_part)
    hidden = (jax.nn.silu(gate) * up_proj).astype(jnp.bfloat16)
    mixed = jnp.dot(
        hidden,
        lax.all_gather(down_part, "user", axis=1, tiled=True),
        preferred_element_type=jnp.float32,
    )
    pooled_mlp = jnp.sum(mixed.reshape(-1, STEPS, width_model), axis=1)
    pooled_mlp = lax.psum_scatter(pooled_mlp, "gen", scatter_dimension=1, tiled=True)
    slab_width = pooled_mlp.shape[1]
    own_cols = lax.dynamic_slice_in_dim(values, lax.axis_index("gen") * slab_width, slab_width, 1)
    pooled_in = jnp.sum(own_cols.reshape(groups, STEPS, slab_width), axis=1)
    pooled = ((pooled_in + pooled_mlp) / STEPS).astype(jnp.bfloat16)
    partial_emb = jnp.dot(pooled, proj_weight, preferred_element_type=jnp.float32)
    embedding = lax.psum(partial_emb, "gen")
    candidate = unit_rows(embedding)
    every_cand = lax.all_gather(candidate, "user", axis=0, tiled=True)
    encoded = unit_rows(jnp.dot(private_rows, enc_weight, preferred_element_type=jnp.float32))
    scores = lax.dot_general(
        encoded, every_cand, (((1,), (1,)), ((), ())), preferred_element_type=jnp.float32
    )
    kernel = jnp.exp(scores * 60.0)
    totals = lax.psum(jnp.sum(kernel, axis=1), "cand")
    member = (user_ids[:, None] == jnp.arange(USERS_DEV, dtype=jnp.int32)[None, :]).astype(
        jnp.float32
    )
    counts = jnp.sum(member, axis=0)
    limit = jnp.minimum(1.0, CAP / jnp.maximum(counts, 1.0))
    row_cap = jnp.dot(member, limit, precision=lax.Precision.HIGHEST)
    row_total = private_rows.shape[0] * lax.axis_size("gen") * lax.axis_size("user")
    cand_total = every_cand.shape[0] * lax.axis_size("cand")
    weight_rows = row_cap / totals * (cand_total / row_total)
    partial_votes = jnp.dot(weight_rows, kernel, precision=lax.Precision.HIGHEST)
    votes = lax.psum(partial_votes, ("gen", "user"))
    return votes.reshape(lax.axis_size("user"), 1, groups)


def solution(mesh):
    return jax.shard_map(
        shards,
        mesh=mesh,
        in_specs=(
            P(("user", "cand"), None),
            P(),
            P("user", "gen"),
            P("user", "gen"),
            P("gen", "user"),
            P("gen", None),
            P(("gen", "user"), None),
            P(),
            P(("gen", "user")),
        ),
        out_specs=P(None, "cand", None),
        check_vma=False,
    )
```

profile of v0, /device:TPU:0, one launch (start us, length us, event | category | flops | bytes accessed | tf_op | source)
XLA Modules:
  0.0 810.1 jit_solution(10870717847516051505)
XLA Ops:
  6.5 0.0 copy-start
  6.5 0.0 copy-start.1
  6.5 0.0 all-gather.5.cloned.1.call-start
  6.5 0.7 all-gather.5.cloned.1.call-update
  7.3 0.0 all-gather.7.cloned.1.call-start
  7.3 0.7 all-gather.7.cloned.1.call-update
  8.0 0.0 all-gather.9.cloned.1.call-start
  8.1 0.7 all-gather.9.cloned.1.call-update
  8.7 0.0 reduce-scatter.2.cloned.1.call-start
  8.8 3.1 multiply_reduce_fusion
  11.9 70.3 %all-gather.5.cloned.1.call-done = bf16[4096,896]{1,0:T(8,128)(2,1)} async-done(((bf16[256,896]{1,0:T(8,128)(2,1)}), bf16[4096,896]{1,0:T(8,128)(2,1)}) %all-gather.5.cloned.1.call-update) | async-done | bytes 7340048 | tf_op jit(solution)/shard_map/all_gather | solution.py:22
  82.2 0.0 copy-done.1
  82.2 10.1 %fusion.1 = f32[512,896]{1,0:T(8,128)} fusion(bf16[4096,896]{1,0:T(8,128)(2,1)} %all-gather.5.cloned.1.call-done, f32[4096]{0:T(1024)S(1)} %copy-done.1, f32[512]{0:T(512)S(1)} %add_rsqrt_fusion, bf16[512,4096]{1,0:T(8,128)(2,1)} %param.9), kind=kOutput, calls=%fused_computation.5 | convolution fusion | flops 3766484992 | bytes 13387776 | tf_op jit(solution)/shard_map/dot_general | solution.py:20
  92.3 63.2 %all-gather.7.cloned.1.call-done = bf16[4096,896]{1,0:T(8,128)(2,1)} async-done(((bf16[256,896]{1,0:T(8,128)(2,1)}), bf16[4096,896]{1,0:T(8,128)(2,1)}) %all-gather.7.cloned.1.call-update) | async-done | bytes 7340048 | tf_op jit(solution)/shard_map/all_gather | solution.py:23
  155.6 79.3 %all-gather.9.cloned.1.call-done = bf16[896,4096]{1,0:T(8,128)(2,1)} async-done(((bf16[896,256]{1,0:T(8,128)(2,1)}), bf16[896,4096]{1,0:T(8,128)(2,1)}) %all-gather.9.cloned.1.call-update) | async-done | bytes 7340048 | tf_op jit(solution)/shard_map/all_gather | solution.py:49
  234.8 17.4 %fusion.2 = f32[512,4096]{1,0:T(8,128)} fusion(bf16[896,4096]{1,0:T(8,128)(2,1)} %all-gather.9.cloned.1.call-done, f32[512,896]{1,0:T(8,128)} %fusion.1, bf16[4096,896]{1,0:T(8,128)(2,1)} %all-gather.7.cloned.1.call-done, f32[4096]{0:T(1024)S(1)} %copy-done.1, f32[512]{0:T(512)S(1)} %add_rsqrt_fusion, bf16[512,4096]{1,0:T(8,128)(2,1)} %param.9), kind=kOutput, calls=%fused_computation.9 | convolution fusion | flops 7527333888 | bytes 29116416 | tf_op jit(solution)/shard_map/dot_general | solution.py:47
  252.2 9.8 %reshape.32 = f32[128,4,4096]{2,1,0:T(4,128)} reshape(f32[512,4096]{1,0:T(8,128)} %fusion.2) | data formatting | bytes 16777216 | tf_op jit(solution)/shard_map/reshape | solution.py:52
  262.0 10.0 %reduce_sum.67 = f32[128,4096]{1,0:T(8,128)} reduce(f32[128,4,4096]{2,1,0:T(4,128)} %reshape.32, f32[]{:T(128)} %constant.15.clone.1), dimensions={1}, to_apply=%region_4.5 | reduce | flops 1572864 | bytes 10485764 | tf_op jit(solution)/shard_map/reduce_sum | solution.py:52
  272.0 0.0 reduce-scatter.2.cloned.1.call-update
  272.1 0.0 all-reduce.2.cloned.1.call-start
  272.1 6.5 convert_element_type.23
  278.6 1.3 constant_dynamic-slice_fusion
  279.9 0.0 copy-start.2
  279.9 1.3 reshape.31
  281.2 1.8 reduce_sum.65
  283.1 29.9 %reduce-scatter.2.cloned.1.call-done = f32[128,512]{1,0:T(8,128)} async-done(((f32[128,4096]{1,0:T(8,128)}), f32[128,512]{1,0:T(8,128)}) %reduce-scatter.2.cloned.1.call-update) | async-done | bytes 262160 | tf_op jit(solution)/shard_map/reduce_scatter | solution.py:53
  313.0 2.4 fusion.4
  315.4 0.0 all-reduce.2.cloned.1.call-update
  315.4 0.3 all-gather.11.cloned.1.call-start
  315.7 70.7 %all-reduce.2.cloned.1.call-done = f32[128,1024]{1,0:T(8,128)} async-done(((f32[128,1024]{1,0:T(8,128)}), f32[128,1024]{1,0:T(8,128)}) %all-reduce.2.cloned.1.call-update) | async-done | bytes 524304 | tf_op jit(solution)/shard_map/psum | solution.py:59
  386.3 1.2 multiply_reduce_fusion.2
  387.5 1.8 multiply_convert_fusion.8
  389.3 0.0 all-gather.11.cloned.1.call-update
  389.4 0.0 copy-done.2
  389.4 0.1 convert_reduce_fusion
  389.5 0.0 copy-done
  389.5 1.8 multiply_reduce_fusion.1
  391.3 0.1 fusion.6
  391.5 53.5 %all-gather.11.cloned.1.call-done = bf16[2048,1024]{1,0:T(8,128)(2,1)} async-done(((bf16[128,1024]{1,0:T(8,128)(2,1)}), bf16[2048,1024]{1,0:T(8,128)(2,1)}) %all-gather.11.cloned.1.call-update) | async-done | bytes 4194320 | tf_op jit(solution)/shard_map/all_gather | solution.py:61
  445.0 4.9 fusion.16
  449.8 8.8 %psum.22 = f32[256]{0:T(256)S(1)} all-reduce(f32[256]{0:T(256)S(1)} %get-tuple-element.7), channel_id=1, replica_groups=mesh['gen'=8,'user'=16,'cand'=2] {'cand'}, use_global_device_ids=true, to_apply=%region_9.10 | all-reduce | flops 256 | bytes 2048 | tf_op jit(solution)/shard_map/psum | solution.py:67
  458.6 2.7 convolution_bitcast_fusion
  461.3 341.9 %psum.23 = f32[16,1,128]{2,1,0:T(1,128)} all-reduce(f32[16,1,128]{2,1,0:T(1,128)S(1)} %convolution_bitcast_fusion), channel_id=1, replica_groups=mesh['gen'=8,'user'=16,'cand'=2] {'gen','user'}, use_global_device_ids=true, to_apply=%region_10.11 | all-reduce | flops 2048 | bytes 16384 | tf_op jit(solution)/shard_map/psum | solution.py:78
  (4 shorter events, 0.0 us)
Async XLA Ops:
  6.5 383.0 %copy-start = (bf16[1024,1024]{1,0:T(8,128)(2,1)S(1)}, bf16[1024,1024]{1,0:T(8,128)(2,1)}, u32[]{:S(2)}) copy-start(bf16[1024,1024]{1,0:T(8,128)(2,1)} %param.16) | copy-start | bytes 6291460
  6.5 75.7 %copy-start.1 = (f32[4096]{0:T(1024)S(1)}, f32[4096]{0:T(1024)}, u32[]{:S(2)}) copy-start(f32[4096]{0:T(1024)} %param.10) | copy-start | bytes 49156
  6.5 75.7 %all-gather.5.cloned.1.call-start = ((), (), s32[]{:S(2)}) async-start(), calls=%async_computation.1 | async-start | bytes 7798784 | tf_op jit(solution)/shard_map/all_gather | solution.py:22
  7.3 148.3 %all-gather.7.cloned.1.call-start = ((), (), s32[]{:S(2)}) async-start(), calls=%async_computation.2 | async-start | bytes 7798784 | tf_op jit(solution)/shard_map/all_gather | solution.py:23
  8.0 226.8 %all-gather.9.cloned.1.call-start = ((), (), s32[]{:S(2)}) async-start(), calls=%async_computation.3 | async-start | bytes 7798784 | tf_op jit(solution)/shard_map/all_gather | solution.py:49
  8.7 304.2 %reduce-scatter.2.cloned.1.call-start = ((), (), s32[]{:S(2)}) async-start(), calls=%async_computation.4 | async-start | bytes 2359296 | tf_op jit(solution)/shard_map/reduce_scatter | solution.py:53
  272.1 114.3 %all-reduce.2.cloned.1.call-start = ((), (), s32[]{:S(2)}) async-start(), calls=%async_computation.5 | async-start | bytes 1048576 | tf_op jit(solution)/shard_map/psum | solution.py:59
  279.9 109.5 %copy-start.2 = (s32[256]{0:T(256)S(1)}, s32[256]{0:T(256)}, u32[]{:S(2)}) copy-start(s32[256]{0:T(256)} %param.17) | copy-start | bytes 3076
  315.4 129.5 %all-gather.11.cloned.1.call-start = ((), (), s32[]{:S(2)}) async-start(), calls=%async_computation.6 | async-start | bytes 4456448 | tf_op jit(solution)/shard_map/all_gather | solution.py:61
Sparse Core Ops, SparseCore 0:
  9.8 72.3 all-gather.4
  84.7 70.8 all-gather.6
  158.0 76.7 all-gather.8
  272.2 40.7 reduce-scatter.1
  315.5 70.7 all-reduce.1
  389.5 55.4 all-gather.10
where the time goes:
time: 811 us; the launch traced here: 810 us
  waiting for transfers between devices  369 us (45%)
  blocking collectives  351 us (43%)
  matrix products  39.5 us (5%)
  other arithmetic  24.6 us (3%)
  between operations  13.5 us (2%)
  local copies, waits for them, and re-layouts  12.4 us (2%)
    psum x1, blocking collectives, shards(): votes = lax.psum(partial_votes, ('gen', 'user'))  342 us
    all_gather x1, waiting for transfers between devices, shards(): lax.all_gather(down_part, 'user', axis=1, tiled=True)  79.3 us
    psum x1, waiting for transfers between devices, shards(): embedding = lax.psum(partial_emb, 'gen')  70.7 us
    all_gather x1, waiting for transfers between devices, project_in(): gate = add_rows(lax.all_gather(gate_part, 'user', axis=0, tiled=True))  70.3 us
    all_gather x1, waiting for transfers between devices, project_in(): up_proj = add_rows(lax.all_gather(up_part, 'user', axis=0, tiled=True))  63.2 us
    all_gather x1, waiting for transfers between devices, shards(): every_cand = lax.all_gather(candidate, 'user', axis=0, tiled=True)  53.5 us
    reduce_scatter x1, waiting for transfers between devices, shards(): lax.psum_scatter(pooled_mlp, 'gen', scatter_dimension=1, tiled=True)  29.9 us
    dot_general x1, matrix products, shards(): jnp.dot(hidden, lax.all_gather(down_part, 'user', axis=1, tiled=True), pr...  17.4 us
  transfers between devices with their start and end apart: 6, of which 6 were waited for; matrix products, arithmetic and copies ran while one was open for 3% of the time, Pallas kernels for 0%

commit v1 on v0

--- a/solution.py
+++ b/solution.py
@@ -46,7 +46,7 @@
     hidden = (jax.nn.silu(gate) * up_proj).astype(jnp.bfloat16)
     mixed = jnp.dot(
         hidden,
-        lax.all_gather(down_part, "user", axis=1, tiled=True),
+        jnp.concatenate(lax.all_gather(down_part, "user"), axis=1),
         preferred_element_type=jnp.float32,
     )
     pooled_mlp = jnp.sum(mixed.reshape(-1, STEPS, width_model), axis=1)

time: 811 us -> 789 us (0.973)
  waiting for transfers between devices: 369 us -> 351 us
  other arithmetic: 24.6 us -> 14.6 us
    all_gather x1, waiting for transfers between devices: 79.3 us -> 61.3 us  [shards(): lax.all_gather(down_part, 'user')]
    dot_general x1 -> x2, matrix products: 10.1 us -> 20.4 us  [add_rows(): return jnp.dot(inputs, piece, preferred_element_type=jnp.float32)]
    reduce_sum x1 -> x0, other arithmetic: 10 us -> none  [shards(): pooled_mlp = jnp.sum(mixed.reshape(-1, STEPS, width_model), axis=1)]
  transfers between devices with their start and end apart: 6 -> 6, of which waited for: 6 -> 6; matrix products, arithmetic and copies ran while one was open for 3% -> 5% of each run, Pallas kernels for 0% -> 0%
where the time goes in v1:
time: 789 us; the launch traced here: 788 us
  waiting for transfers between devices  351 us (44%)
  blocking collectives  351 us (44%)
  matrix products  41.7 us (5%)
  local copies, waits for them, and re-layouts  15.5 us (2%)
  other arithmetic  14.6 us (2%)
  between operations  13.5 us (2%)
    psum x1, blocking collectives, shards(): votes = lax.psum(partial_votes, ('gen', 'user'))  342 us
    psum x1, waiting for transfers between devices, shards(): embedding = lax.psum(partial_emb, 'gen')  71.1 us
    all_gather x1, waiting for transfers between devices, project_in(): gate = add_rows(lax.all_gather(gate_part, 'user', axis=0, tiled=True))  70.3 us
    all_gather x1, waiting for transfers between devices, project_in(): up_proj = add_rows(lax.all_gather(up_part, 'user', axis=0, tiled=True))  63.2 us
    all_gather x1, waiting for transfers between devices, shards(): lax.all_gather(down_part, 'user')  61.3 us
    all_gather x1, waiting for transfers between devices, shards(): every_cand = lax.all_gather(candidate, 'user', axis=0, tiled=True)  53.5 us
    reduce_scatter x1, waiting for transfers between devices, shards(): lax.psum_scatter(pooled_mlp, 'gen', scatter_dimension=1, tiled=True)  30 us
    dot_general x2, matrix products, add_rows(): return jnp.dot(inputs, piece, preferred_element_type=jnp.float32)  20.4 us
  transfers between devices with their start and end apart: 6, of which 6 were waited for; matrix products, arithmetic and copies ran while one was open for 5% of the time, Pallas kernels for 0%

profile of v1, /device:TPU:0, one launch (start us, length us, event | category | flops | bytes accessed | tf_op | source)
XLA Modules:
  0.0 787.9 jit_solution(11399392616675531968)
XLA Ops:
  6.5 0.0 copy-start
  6.5 0.0 copy-start.1
  6.5 0.0 all-gather.6.cloned.1.call-start
  6.5 0.7 all-gather.6.cloned.1.call-update
  7.3 0.0 all-gather.8.cloned.1.call-start
  7.3 0.7 all-gather.8.cloned.1.call-update
  8.0 0.0 all-gather.12.cloned.1.call-start
  8.1 0.7 all-gather.12.cloned.1.call-update
  8.7 0.0 reduce-scatter.2.cloned.1.call-start
  8.8 3.1 multiply_reduce_fusion
  11.9 70.3 %all-gather.6.cloned.1.call-done = bf16[4096,896]{1,0:T(8,128)(2,1)} async-done(((bf16[256,896]{1,0:T(8,128)(2,1)}), bf16[4096,896]{1,0:T(8,128)(2,1)}) %all-gather.6.cloned.1.call-update) | async-done | bytes 7340048 | tf_op jit(solution)/shard_map/all_gather | solution.py:22
  82.2 0.0 copy-done.1
  82.2 10.2 %fusion.1 = f32[512,896]{1,0:T(8,128)} fusion(bf16[4096,896]{1,0:T(8,128)(2,1)} %all-gather.6.cloned.1.call-done, f32[4096]{0:T(1024)S(1)} %copy-done.1, f32[512]{0:T(512)S(1)} %add_rsqrt_fusion, bf16[512,4096]{1,0:T(8,128)(2,1)} %param.9), kind=kOutput, calls=%fused_computation.6 | convolution fusion | flops 3766484992 | bytes 13387776 | tf_op jit(solution)/shard_map/dot_general | solution.py:20
  92.4 63.2 %all-gather.8.cloned.1.call-done = bf16[4096,896]{1,0:T(8,128)(2,1)} async-done(((bf16[256,896]{1,0:T(8,128)(2,1)}), bf16[4096,896]{1,0:T(8,128)(2,1)}) %all-gather.8.cloned.1.call-update) | async-done | bytes 7340048 | tf_op jit(solution)/shard_map/all_gather | solution.py:23
  155.6 10.3 %multiply_convert_fusion.1 = bf16[512,896]{1,0:T(8,128)(2,1)} fusion(f32[512,896]{1,0:T(8,128)} %fusion.1, bf16[4096,896]{1,0:T(8,128)(2,1)} %all-gather.8.cloned.1.call-done, f32[4096]{0:T(1024)S(1)} %copy-done.1, f32[512]{0:T(512)S(1)} %add_rsqrt_fusion, bf16[512,4096]{1,0:T(8,128)(2,1)} %param.9), kind=kOutput, calls=%fused_computation.5 | convolution fusion | flops 3769237504 | bytes 14305280 | tf_op jit(solution)/shard_map/dot_general | solution.py:20
  165.8 1.8 dot_general.30
  167.6 61.3 %all-gather.12.cloned.1.call-done = bf16[14336,256]{1,0:T(8,128)(2,1)} async-done(((bf16[896,256]{1,0:T(8,128)(2,1)}), bf16[14336,256]{1,0:T(8,128)(2,1)}) %all-gather.12.cloned.1.call-update) | async-done | bytes 7340048 | tf_op jit(solution)/shard_map/all_gather | solution.py:49
  228.9 11.1 %copy.13 = bf16[896,16,256]{0,2,1:T(8,128)(2,1)} copy(bf16[896,16,256]{2,0,1:T(8,128)(2,1)} %bitcast.24) | data formatting | bytes 14680064 | tf_op jit(solution)/shard_map/reshape | solution.py:49
  240.1 9.3 %convolution_reduce_fusion = f32[128,4096]{1,0:T(8,128)} fusion(bf16[896,4096,1]{0,1,2:T(8,128)(2,1)} %bitcast.25, bf16[128,4,896]{2,1,0:T(4,128)(2,1)S(1)} %dot_general.30), kind=kOutput, calls=%fused_computation.4 | convolution fusion | flops 3759669248 | bytes 10354688 | tf_op jit(solution)/shard_map/dot_general | solution.py:47
  249.4 0.0 reduce-scatter.2.cloned.1.call-update
  249.4 0.2 all-reduce.2.cloned.1.call-start
  249.6 6.5 convert_element_type.23
  256.1 1.3 constant_dynamic-slice_fusion
  257.4 0.0 copy-start.2
  257.4 1.3 reshape.36
  258.7 1.8 reduce_sum.65
  260.6 30.0 %reduce-scatter.2.cloned.1.call-done = f32[128,512]{1,0:T(8,128)} async-done(((f32[128,4096]{1,0:T(8,128)}), f32[128,512]{1,0:T(8,128)}) %reduce-scatter.2.cloned.1.call-update) | async-done | bytes 262160 | tf_op jit(solution)/shard_map/reduce_scatter | solution.py:53
  290.6 2.4 fusion.4
  293.0 0.0 all-reduce.2.cloned.1.call-update
  293.0 0.0 all-gather.10.cloned.1.call-start
  293.1 71.1 %all-reduce.2.cloned.1.call-done = f32[128,1024]{1,0:T(8,128)} async-done(((f32[128,1024]{1,0:T(8,128)}), f32[128,1024]{1,0:T(8,128)}) %all-reduce.2.cloned.1.call-update) | async-done | bytes 524304 | tf_op jit(solution)/shard_map/psum | solution.py:59
  364.2 1.2 multiply_reduce_fusion.2
  365.3 1.8 multiply_convert_fusion.6
  367.2 0.0 all-gather.10.cloned.1.call-update
  367.2 0.0 copy-done.2
  367.2 0.1 convert_reduce_fusion
  367.3 0.0 copy-done
  367.3 1.8 multiply_reduce_fusion.1
  369.2 0.1 fusion.6
  369.3 53.5 %all-gather.10.cloned.1.call-done = bf16[2048,1024]{1,0:T(8,128)(2,1)} async-done(((bf16[128,1024]{1,0:T(8,128)(2,1)}), bf16[2048,1024]{1,0:T(8,128)(2,1)}) %all-gather.10.cloned.1.call-update) | async-done | bytes 4194320 | tf_op jit(solution)/shard_map/all_gather | solution.py:61
  422.8 4.9 fusion.15
  427.6 8.8 %psum.22 = f32[256]{0:T(256)S(1)} all-reduce(f32[256]{0:T(256)S(1)} %get-tuple-element.7), channel_id=1, replica_groups=mesh['gen'=8,'user'=16,'cand'=2] {'cand'}, use_global_device_ids=true, to_apply=%region_9.10 | all-reduce | flops 256 | bytes 2048 | tf_op jit(solution)/shard_map/psum | solution.py:67
  436.5 2.7 convolution_bitcast_fusion
  439.1 341.9 %psum.23 = f32[16,1,128]{2,1,0:T(1,128)} all-reduce(f32[16,1,128]{2,1,0:T(1,128)S(1)} %convolution_bitcast_fusion), channel_id=1, replica_groups=mesh['gen'=8,'user'=16,'cand'=2] {'gen','user'}, use_global_device_ids=true, to_apply=%region_10.11 | all-reduce | flops 2048 | bytes 16384 | tf_op jit(solution)/shard_map/psum | solution.py:78
  (4 shorter events, 0.0 us)
Async XLA Ops:
  6.5 360.8 %copy-start = (bf16[1024,1024]{1,0:T(8,128)(2,1)S(1)}, bf16[1024,1024]{1,0:T(8,128)(2,1)}, u32[]{:S(2)}) copy-start(bf16[1024,1024]{1,0:T(8,128)(2,1)} %param.16) | copy-start | bytes 6291460
  6.5 75.7 %copy-start.1 = (f32[4096]{0:T(1024)S(1)}, f32[4096]{0:T(1024)}, u32[]{:S(2)}) copy-start(f32[4096]{0:T(1024)} %param.10) | copy-start | bytes 49156
  6.5 75.7 %all-gather.6.cloned.1.call-start = ((), (), s32[]{:S(2)}) async-start(), calls=%async_computation.1 | async-start | bytes 7798784 | tf_op jit(solution)/shard_map/all_gather | solution.py:22
  7.3 148.3 %all-gather.8.cloned.1.call-start = ((), (), s32[]{:S(2)}) async-start(), calls=%async_computation.2 | async-start | bytes 7798784 | tf_op jit(solution)/shard_map/all_gather | solution.py:23
  8.0 220.9 %all-gather.12.cloned.1.call-start = ((), (), s32[]{:S(2)}) async-start(), calls=%async_computation.6 | async-start | bytes 7798784 | tf_op jit(solution)/shard_map/all_gather | solution.py:49
  8.7 281.8 %reduce-scatter.2.cloned.1.call-start = ((), (), s32[]{:S(2)}) async-start(), calls=%async_computation.3 | async-start | bytes 2359296 | tf_op jit(solution)/shard_map/reduce_scatter | solution.py:53
  249.4 114.8 %all-reduce.2.cloned.1.call-start = ((), (), s32[]{:S(2)}) async-start(), calls=%async_computation.4 | async-start | bytes 1048576 | tf_op jit(solution)/shard_map/psum | solution.py:59
  257.4 109.8 %copy-start.2 = (s32[256]{0:T(256)S(1)}, s32[256]{0:T(256)}, u32[]{:S(2)}) copy-start(s32[256]{0:T(256)} %param.17) | copy-start | bytes 3076
  293.0 129.7 %all-gather.10.cloned.1.call-start = ((), (), s32[]{:S(2)}) async-start(), calls=%async_computation.5 | async-start | bytes 4456448 | tf_op jit(solution)/shard_map/all_gather | solution.py:61
Sparse Core Ops, SparseCore 0:
  9.8 72.3 all-gather.5
  84.7 70.8 all-gather.7
  158.1 70.8 all-gather.11
  249.5 41.0 reduce-scatter.1
  293.2 70.9 all-reduce.1
  367.3 55.4 all-gather.9
